TPU v7x, 32 devices: a whole 2x2x4 slice. The times are simulated.
32 devices in a mesh: section: 2 (over x), view: 8 (over z, y), scene: 2 (over core).
Axes of the slice: x: 2, y: 2, z: 4, core: 2. Of those that a mesh axis runs over, the one named last changes fastest.
Arguments:
- tokens: bfloat16 [2, 512, 1024], P('scene', ('section', 'view')), may hold values from -6 to 6
- norm_gain: float32 [1024], replicated, may hold values from 0.1 to 1.9
- head_weight: bfloat16 [1024, 512], replicated, may hold values from -0.1875 to 0.1875
- tile_lists: int32 [2, 64, 128], P('scene', ('section', 'view')), may hold values from 0 to 32767, as said below
- tile_counts: int32 [2, 64], P('scene', ('section', 'view')), may hold values from 1 to 128, as said below
- cameras: float32 [2, 2, 8], P('scene'), may hold values from -3 to 3
- targets: bfloat16 [2, 64, 768], P('scene', ('section', 'view')), may hold values from 0 to 1
Outputs:
- image: bfloat16 [2, 64, 768], P('scene', ('section', 'view'))
- grad_head: float32 [1024, 512], replicated
- loss: float32 [], replicated
Inputs may be any that keep to these rules, and one draw needn't show every extreme that they name: `tile_lists`: gaussian n of a scene has owner n // 2048. Among the 512 slots (live or not) of each aligned block of 4 tiles, at most 64 name Gaussians of one owner, and in every such block some owner is named exactly 64 times. `tile_counts`: the first tile of each scene has 128 live slots.
All inputs are finite; a program needn't handle non-finite values.
Results may differ from a plain program's by a relative error of at most 0.014.
Values may be sent and summed in bfloat16 or wider, within the bound.
A program may use at most 256 MiB of HBM per device.

v0:
```python
import jax
import jax.numpy as jnp
from jax import lax
from jax.sharding import PartitionSpec as P

GPT = 64
PARAMS = 8
K = 128
SIDE = 16
VIEWS = 2


def pixel_grid():
    place = jnp.arange(SIDE * SIDE, dtype=jnp.int32)
    across = ((place % SIDE).astype(jnp.float32) + 0.5) * (2.0 / SIDE) - 1.0
    down = ((place // SIDE).astype(jnp.float32) + 0.5) * (2.0 / SIDE) - 1.0
    return (across, down)


def composite(values, live, cams, wanted, across, down):
    slots = jnp.arange(K, dtype=jnp.int32)
    strict = (slots[:, None] < slots[None, :]).astype(jnp.float32)
    sx = jnp.tanh(
        cams[:, 0:1] * values[0]
        + cams[:, 1:2] * values[1]
        + cams[:, 2:3] * values[2]
        + cams[:, 3:4]
    )
    sy = jnp.tanh(
        cams[:, 4:5] * values[0]
        + cams[:, 5:6] * values[1]
        + cams[:, 6:7] * values[2]
        + cams[:, 7:8]
    )
    spread = jnp.exp(-2.0 * values[3])
    dxx = across[None, None, :] - sx[:, :, None]
    dyy = down[None, None, :] - sy[:, :, None]
    alpha = (
        0.3
        * jax.nn.sigmoid(values[4])[:, :, None]
        * jnp.exp(-0.5 * (dxx * dxx + dyy * dyy) * spread[:, :, None])
        * live[:, :, None]
    )
    logs = jnp.log1p(-alpha)
    before = jnp.einsum("bkp,kj->bjp", logs, strict, precision=lax.Precision.HIGHEST)
    weight = alpha * jnp.exp(before)
    colour = jnp.einsum(
        "bkp,cbk->bcp", weight, jax.nn.sigmoid(values[5:8]), precision=lax.Precision.HIGHEST
    )
    colour = colour.reshape(colour.shape[0], 3 * SIDE * SIDE)
    diff = colour - wanted.astype(jnp.float32)
    return (jnp.sum(diff * diff), colour)


def to_gauss(head, rows):
    return (
        head.reshape(rows, PARAMS, GPT)
        .transpose(1, 0, 2)
        .reshape(PARAMS, rows * GPT)
        .astype(jnp.bfloat16)
    )


def body(tokens, norm_gain, head_weight, tile_lists, tile_counts, cameras, targets):
    tok_rows = tokens.shape[1]
    tile_rows = tile_lists.shape[1]
    group = lax.axis_size(("section", "view"))
    scenes_all = lax.axis_size("scene")
    tiles_all = tile_rows * group
    factor = 1.0 / (scenes_all * tiles_all)
    values_in = tokens[0].astype(jnp.float32)
    scale = lax.rsqrt(jnp.mean(values_in * values_in, axis=-1, keepdims=True) + 1e-06)
    normed = (values_in * scale * norm_gain).astype(jnp.bfloat16)
    lists = tile_lists[0]
    own_count = tok_rows * GPT
    slot_total = tile_rows * K
    bucket = 2 * ((slot_total + group - 1) // group)
    flat = lists.reshape(-1)
    owner = flat // own_count
    inner = flat - owner * own_count
    order = jnp.argsort(owner, stable=True)
    sorted_owner = owner[order]
    owner_ids = jnp.arange(group, dtype=jnp.int32)
    per_owner = jnp.sum((owner[:, None] == owner_ids[None, :]).astype(jnp.int32), axis=0)
    starts = jnp.cumsum(per_owner) - per_owner
    rank = jnp.arange(slot_total, dtype=jnp.int32) - starts[sorted_owner]
    target_slot = jnp.zeros((slot_total,), jnp.int32).at[order].set(sorted_owner * bucket + rank)
    wanted_rows = (
        jnp.zeros((group * bucket,), jnp.int32).at[target_slot].set(inner).reshape(group, bucket)
    )
    asked = lax.all_to_all(
        wanted_rows, ("section", "view"), split_axis=0, concat_axis=0, tiled=True
    )
    head = jnp.dot(normed, head_weight, preferred_element_type=jnp.float32)
    own_gauss = to_gauss(head, tok_rows)
    answer = (
        jnp.take(own_gauss, asked.reshape(-1), axis=1)
        .reshape(PARAMS, group, bucket)
        .transpose(1, 0, 2)
    )
    received = lax.all_to_all(answer, ("section", "view"), split_axis=0, concat_axis=0, tiled=True)
    table = received.transpose(1, 0, 2).reshape(PARAMS, group * bucket).astype(jnp.float32)
    values = jnp.take(table, target_slot, axis=1).reshape(PARAMS, tile_rows, K)
    per_view = tiles_all // VIEWS
    first_tile = lax.axis_index(("section", "view")) * tile_rows
    which = (first_tile + jnp.arange(tile_rows, dtype=jnp.int32)) // per_view
    onehot = (which[:, None] == jnp.arange(VIEWS, dtype=jnp.int32)[None, :]).astype(jnp.float32)
    tile_cams = jnp.dot(onehot, cameras[0], precision=lax.Precision.HIGHEST)
    slots = jnp.arange(K, dtype=jnp.int32)
    live = (slots[None, :] < tile_counts[0][:, None]).astype(jnp.float32)
    across, down = pixel_grid()

    def local(vals):
        return composite(vals, live, tile_cams, targets[0], across, down)

    part, pullback, colour = jax.vjp(local, values, has_aux=True)
    grads = pullback(jnp.ones_like(part) * factor)[0]
    outgoing = (
        jnp.zeros((PARAMS, group * bucket), jnp.float32)
        .at[:, target_slot]
        .set(grads.reshape(PARAMS, -1))
    )
    outgoing = outgoing.reshape(PARAMS, group, bucket).transpose(1, 0, 2)
    returned = lax.all_to_all(
        outgoing.astype(jnp.bfloat16), ("section", "view"), split_axis=0, concat_axis=0, tiled=True
    ).astype(outgoing.dtype)
    own = (
        jnp.zeros((PARAMS, own_count), jnp.float32)
        .at[:, asked.reshape(-1)]
        .add(returned.transpose(1, 0, 2).reshape(PARAMS, -1))
    )
    dhead = own.reshape(PARAMS, tok_rows, GPT).transpose(1, 0, 2).reshape(tok_rows, PARAMS * GPT)
    partial_grad = jnp.dot(normed.astype(jnp.float32).T, dhead, precision=lax.Precision.HIGHEST)
    grad_head, loss = lax.psum((partial_grad, part * factor), ("section", "view", "scene"))
    return (colour.astype(jnp.bfloat16)[None], grad_head, loss)


def solution(mesh):
    in_specs = (
        P("scene", ("section", "view"), None),
        P(),
        P(),
        P("scene", ("section", "view"), None),
        P("scene", ("section", "view")),
        P("scene", None, None),
        P("scene", ("section", "view"), None),
    )
    out_specs = (P("scene", ("section", "view"), None), P(), P())
    return jax.shard_map(body, mesh=mesh, in_specs=in_specs, out_specs=out_specs, check_vma=False)
```

profile of v0, /device:TPU:0, one launch (start us, length us, event | category | flops | bytes accessed | tf_op | source)
XLA Modules:
  0.0 234.9 jit_solution(6555050550553904931)
XLA Ops:
  7.2 0.0 copy-start
  7.2 0.8 bitcast_subtract_fusion
  8.0 0.1 convert_reduce_fusion
  8.1 3.8 %sort.17 = (s32[512]{0:T(512)}, s32[512]{0:T(512)S(1)}) sort(s32[512]{0:T(512)S(1)} %get-tuple-element.51, s32[512]{0:T(512)S(1)} %iota.50), dimensions={0}, to_apply=%region_0.0 | sort | flops 4608 | bytes 8192 | tf_op jit(solution)/shard_map/jit(argsort)/sort | solution.py:81
  11.9 0.0 copy-start.3
  11.9 3.5 %gather_fusion = s32[512]{0:T(512)S(1)} fusion(s32[512]{0:T(512)S(1)} %get-tuple-element.51, s32[1024]{0:T(1024)S(1)} %pad_clamp_fusion.1), kind=kCustom, calls=%fused_computation | custom fusion | bytes 6144 | tf_op jit(solution)/shard_map/gather | solution.py:82
  15.4 0.1 copy.121
  15.6 0.1 reduce.3
  15.7 0.7 fusion.106
  16.4 4.3 %compare_select_fusion.3 = (s32[512,1]{0,1:T(1,128)S(1)}, s32[512,1]{0,1:T(1,128)S(1)}) fusion(s32[]{:T(128)} %bitcast.12, s32[]{:T(128)} %bitcast.13, s32[]{:T(128)} %bitcast.14, s32[]{:T(128)} %bitcast.15, s32[]{:T(128)} %bitcast.16, s32[]{:T(128)} %bitcast.18, s32[]{:T(128)} %bitcast.17, s32[512,1]{0,1:T(1,128)S(1)} %bitcast.179), kind=kLoop, calls=%fused_computation.113 | loop fusion | flops 7680 | bytes 6172 | tf_op jit(solution)/shard_map/gather | solution.py:86
  20.7 0.1 compare_reduce_fusion.8
  20.8 5.7 %fusion.82 = s32[512]{0:T(512)S(1)} fusion(pred[512]{0:T(512)(128)(4,1)S(1)} %get-tuple-element.25, pred[512]{0:T(512)(128)(4,1)S(1)} %get-tuple-element.24, pred[512]{0:T(512)(128)(4,1)S(1)} %get-tuple-element.23, pred[512]{0:T(512)(128)(4,1)S(1)} %get-tuple-element.22, pred[512]{0:T(512)(128)(4,1)S(1)} %get-tuple-element.21, ...), kind=kLoop, calls=%fused_computation.148 | loop fusion | flops 6144 | bytes 10788 | tf_op jit(solution)/shard_map/add | solution.py:87
  26.5 2.4 %scatter_custom_fusion = s32[512]{0:T(512)S(1)} fusion(s32[512]{0:T(512)S(1)} %compare_select_fusion.10, s32[512]{0:T(512)S(1)} %fusion.82, s32[]{:T(128)} %constant.112.clone.1), kind=kCustom, calls=%fused_computation.196 | custom fusion | bytes 2052 | tf_op jit(solution)/shard_map/scatter | solution.py:87
  29.0 2.4 %scatter_custom_fusion.1 = s32[1024]{0:T(1024)S(1)} fusion(s32[512]{0:T(512)S(1)} %compare_select_fusion.9, s32[512]{0:T(512)S(1)} %get-tuple-element.50, s32[]{:T(128)} %constant.112.clone.1), kind=kCustom, calls=%fused_computation.162 | custom fusion | bytes 4100 | tf_op jit(solution)/shard_map/scatter | solution.py:89
  31.4 0.7 all_to_all.12
  32.1 8.3 %all-to-all-start = ((s32[16,1,64]{2,1,0:T(1,128)}), s32[16,1,64]{2,1,0:T(1,128)S(1)}, u32[]{:S(2)}, u32[]{:S(2)}) async-start(s32[16,1,64]{2,1,0:T(1,128)} %all_to_all.12), calls=%async_computation | async-start | bytes 16384 | tf_op jit(solution)/shard_map/all_to_all | solution.py:91
  40.5 0.1 fusion.86
  40.6 0.1 fusion.87
  40.7 0.1 fusion.54
  40.8 0.2 fusion.85
  41.0 0.3 slice_reduce_fusion.7
  41.3 0.0 copy-start.4
  41.3 0.5 copy.122
  41.9 0.6 fusion.4
  42.5 0.3 copy.142
  42.8 4.9 %all-to-all-done = s32[16,1,64]{2,1,0:T(1,128)S(1)} async-done(((s32[16,1,64]{2,1,0:T(1,128)}), s32[16,1,64]{2,1,0:T(1,128)S(1)}, u32[]{:S(2)}, u32[]{:S(2)}) %all-to-all-start) | async-done | bytes 4128 | tf_op jit(solution)/shard_map/all_to_all | solution.py:91
  47.7 0.5 broadcast.1157
  48.2 0.7 reduce.40
  48.9 0.1 reshape.1626
  49.0 3.2 %gather_fusion.1 = bf16[1024,8]{1,0:T(8,128)(2,1)S(1)} fusion(bf16[8,2048]{0,1:T(8,128)(2,1)S(1)} %bitcast.162, s32[1024]{0:T(1024)S(1)} %broadcast_clamp_fusion), kind=kCustom, calls=%fused_computation.1 | custom fusion | bytes 36864 | tf_op jit(solution)/shard_map/jit(_take)/gather | solution.py:97
  52.2 0.1 copy.124
  52.4 0.7 reshape.1807
  53.1 3.5 %all-to-all-start.1 = ((bf16[16,2,256]{2,1,0:T(2,128)(2,1)}), bf16[16,2,256]{2,1,0:T(2,128)(2,1)S(1)}, u32[]{:S(2)}, u32[]{:S(2)}) async-start(bf16[16,2,256]{2,1,0:T(2,128)(2,1)} %reshape.1807), calls=%async_computation.1 | async-start | bytes 32768 | tf_op jit(solution)/shard_map/all_to_all | solution.py:101
  56.6 0.0 all-reduce.11.cloned.1.call-start
  56.7 7.2 %all-to-all-done.1 = bf16[16,2,256]{2,1,0:T(2,128)(2,1)S(1)} async-done(((bf16[16,2,256]{2,1,0:T(2,128)(2,1)}), bf16[16,2,256]{2,1,0:T(2,128)(2,1)S(1)}, u32[]{:S(2)}, u32[]{:S(2)}) %all-to-all-start.1) | async-done | bytes 16416 | tf_op jit(solution)/shard_map/all_to_all | solution.py:101
  63.9 0.1 reshape.1808
  64.0 0.2 copy.125
  64.2 1.0 gather_fusion.2
  65.2 0.1 copy.126
  65.4 0.1 add_tanh_fusion.1
  65.5 0.9 convolution_exponential_fusion
  66.4 1.3 multiply_reduce_fusion
  67.7 0.9 fusion.52
  68.6 0.7 fusion.65
  69.3 1.6 fusion.19
  70.9 0.1 broadcast_multiply_fusion.6
  71.0 0.1 broadcast_multiply_fusion.1
  71.1 0.1 copy.134
  71.3 1.8 scatter_custom_fusion.2
  73.1 0.1 copy.135
  73.3 0.1 reshape.1809
  73.4 9.9 %all_to_all.19 = bf16[16,2,256]{2,1,0:T(2,128)(2,1)S(1)} all-to-all(bf16[16,2,256]{2,1,0:T(2,128)(2,1)S(1)} %reshape.1809), channel_id=1, replica_groups=mesh['section'=2,'view'=8,'scene'=2] {'section','view'}, dimensions={0} | all-to-all | bytes 32768 | tf_op jit(solution)/shard_map/all_to_all | solution.py:124
  83.3 0.1 reshape.1810
  83.4 0.1 reshape.1711
  83.5 0.2 copy.137
  83.7 6.7 %scatter_custom_fusion.3 = f32[8,2048]{0,1:T(8,128)S(1)} fusion(s32[1024]{0:T(1024)S(1)} %bitcast.181, f32[1024,8]{1,0:T(8,128)S(1)} %copy.137, f32[]{:T(128)} %constant.123.clone.1), kind=kCustom, calls=%fused_computation.48 | custom fusion | flops 8192 | bytes 65540 | tf_op jit(solution)/shard_map/scatter-add | solution.py:130
  90.4 0.3 copy.138
  90.8 0.1 reshape.1631
  90.9 2.4 %fusion.58 = f32[1024,512]{1,0:T(8,128)} fusion(f32[32,512]{1,0:T(8,128)S(1)} %reshape.1631, bf16[1,32,1024]{2,1,0:T(8,128)(2,1)S(1)} %copy-done.2, f32[1024]{0:T(1024)S(1)} %copy-done.3, f32[32]{0:T(128)S(1)} %add_rsqrt_fusion), kind=kOutput, calls=%fused_computation.76 | convolution fusion | flops 201457664 | bytes 2232448 | tf_op jit(solution)/shard_map/dot_general | solution.py:133
  93.3 0.0 all-reduce.11.cloned.1.call-update
  93.9 38.3 %psum.15 = f32[]{:T(128)} all-reduce(f32[]{:T(128)S(6)} %mul.699), channel_id=1, replica_groups=mesh['section'=2,'view'=8,'scene'=2] {'section','view','scene'}, use_global_device_ids=true, to_apply=%region_14.15 | all-reduce | flops 1 | bytes 8 | tf_op jit(solution)/shard_map/psum | solution.py:134
  132.3 0.6 convert_element_type.110
  132.9 92.1 %all-reduce.11.cloned.1.call-done = f32[1024,512]{1,0:T(8,128)} async-done(((f32[1024,512]{1,0:T(8,128)}), f32[1024,512]{1,0:T(8,128)}) %all-reduce.11.cloned.1.call-update) | async-done | bytes 2097168 | tf_op jit(solution)/shard_map/psum | solution.py:134
  225.0 3.1 %copy.158 = f32[1024,512]{1,0:T(8,128)} copy(f32[1024,512]{1,0:T(8,128)} %all-reduce.11.cloned.1.call-done) | data formatting | bytes 4194304
  (39 shorter events, 0.4 us)
Async XLA Ops:
  7.2 33.6 %copy-start = (f32[1,2,8]{2,1,0:T(2,128)S(1)}, f32[1,2,8]{2,1,0:T(2,128)}, u32[]{:S(2)}) copy-start(f32[1,2,8]{2,1,0:T(2,128)} %param.12) | copy-start | bytes 196
  7.2 33.3 %copy-start.5 = (s32[1,4]{1,0:T(1,128)S(1)}, s32[1,4]{1,0:T(1,128)}, u32[]{:S(2)}) copy-start(s32[1,4]{1,0:T(1,128)} %param.11) | copy-start | bytes 52
  7.2 33.5 %copy-start.2 = (bf16[1,32,1024]{2,1,0:T(8,128)(2,1)S(1)}, bf16[1,32,1024]{2,1,0:T(8,128)(2,1)}, u32[]{:S(2)}) copy-start(bf16[1,32,1024]{2,1,0:T(8,128)(2,1)} %param.7) | copy-start | bytes 196612
  7.2 34.1 %copy-start.1 = (bf16[1024,512]{1,0:T(8,128)(2,1)S(1)}, bf16[1024,512]{1,0:T(8,128)(2,1)}, u32[]{:S(2)}) copy-start(bf16[1024,512]{1,0:T(8,128)(2,1)} %param.9) | copy-start | bytes 3145732
  11.9 30.0 %copy-start.3 = (f32[1024]{0:T(1024)S(1)}, f32[1024]{0:T(1024)}, u32[]{:S(2)}) copy-start(f32[1024]{0:T(1024)} %param.8) | copy-start | bytes 12292
  32.1 15.6 %all-to-all-start = ((s32[16,1,64]{2,1,0:T(1,128)}), s32[16,1,64]{2,1,0:T(1,128)S(1)}, u32[]{:S(2)}, u32[]{:S(2)}) async-start(s32[16,1,64]{2,1,0:T(1,128)} %all_to_all.12), calls=%async_computation | async-start | bytes 16384 | tf_op jit(solution)/shard_map/all_to_all | solution.py:91
  41.3 15.3 %copy-start.4 = (bf16[1,4,768]{2,1,0:T(4,128)(2,1)S(1)}, bf16[1,4,768]{2,1,0:T(4,128)(2,1)}, u32[]{:S(2)}) copy-start(bf16[1,4,768]{2,1,0:T(4,128)(2,1)} %param.13) | copy-start | bytes 18436
  53.1 10.8 %all-to-all-start.1 = ((bf16[16,2,256]{2,1,0:T(2,128)(2,1)}), bf16[16,2,256]{2,1,0:T(2,128)(2,1)S(1)}, u32[]{:S(2)}, u32[]{:S(2)}) async-start(bf16[16,2,256]{2,1,0:T(2,128)(2,1)} %reshape.1807), calls=%async_computation.1 | async-start | bytes 32768 | tf_op jit(solution)/shard_map/all_to_all | solution.py:101
  56.6 168.4 %all-reduce.11.cloned.1.call-start = ((), (), s32[]{:S(2)}) async-start(), calls=%async_computation.3 | async-start | bytes 4194304 | tf_op jit(solution)/shard_map/psum | solution.py:134
Sparse Core Ops, SparseCore 0:
  93.4 131.5 all-reduce.10
where the time goes:
time: 236 us; the launch traced here: 235 us
  waiting for transfers between devices  104 us (44%)
  blocking collectives  48.3 us (20%)
  local copies, waits for them, and re-layouts  23.8 us (10%)
  other arithmetic  23.1 us (10%)
  between operations  15.1 us (6%)
  starting transfers between devices  11.9 us (5%)
  matrix products  8.56 us (4%)
    psum x1, waiting for transfers between devices, body(): lax.psum((partial_grad, part * factor), ('section', 'view', 'scene'))  92.1 us
    psum x1, blocking collectives, body(): lax.psum((partial_grad, part * factor), ('section', 'view', 'scene'))  38.3 us
    all_to_all x1, blocking collectives, body(): lax.all_to_all(outgoing.astype(jnp.bfloat16), ('section', 'view'), split_...  9.91 us
    all_to_all x1, starting transfers between devices, body(): lax.all_to_all(wanted_rows, ('section', 'view'), split_axis=0, concat_axi...  8.34 us
    all_to_all x1, waiting for transfers between devices, body(): lax.all_to_all(answer, ('section', 'view'), split_axis=0, concat_axis=0,...  7.22 us
    scatter-add x1, other arithmetic, body(): own = jnp.zeros((PARAMS, own_count), jnp.float32).at[:, asked.reshape(-1)...  6.72 us
    add x1, other arithmetic, body(): sorted_owner * bucket + rank  5.71 us
    all_to_all x1, waiting for transfers between devices, body(): lax.all_to_all(wanted_rows, ('section', 'view'), split_axis=0, concat_axi...  4.9 us
  transfers between devices with their start and end apart: 3, of which 3 were waited for; matrix products, arithmetic and copies ran while one was open for 1% of the time, Pallas kernels for 0%

commit v1 on v0

--- a/solution.py
+++ b/solution.py
@@ -8,6 +8,10 @@
 K = 128
 SIDE = 16
 VIEWS = 2
+
+
+def create_cube(shard_axis, mesh_name, a0):
+    return lax.psum(lax.psum(a0, axis_name=shard_axis), mesh_name)
 
 
 def pixel_grid():
@@ -131,7 +135,7 @@
     )
     dhead = own.reshape(PARAMS, tok_rows, GPT).transpose(1, 0, 2).reshape(tok_rows, PARAMS * GPT)
     partial_grad = jnp.dot(normed.astype(jnp.float32).T, dhead, precision=lax.Precision.HIGHEST)
-    grad_head, loss = lax.psum((partial_grad, part * factor), ("section", "view", "scene"))
+    grad_head, loss = create_cube(("view", "scene"), "section", a0=(partial_grad, part * factor))
     return (colour.astype(jnp.bfloat16)[None], grad_head, loss)
 
 

time: 236 us -> 263 us (1.11)
  waiting for transfers between devices: 104 us -> 134 us
    psum x1 -> x2, waiting for transfers between devices: 92.1 us -> 122 us  [create_cube(): return lax.psum(lax.psum(a0, axis_name=shard_axis), mesh_name)]
    psum x1 -> x2, blocking collectives: 38.3 us -> 36.4 us  [create_cube(): return lax.psum(lax.psum(a0, axis_name=shard_axis), mesh_name)]
  transfers between devices with their start and end apart: 3 -> 4, of which waited for: 3 -> 4; matrix products, arithmetic and copies ran while one was open for 1% -> 1% of each run, Pallas kernels for 0% -> 0%
where the time goes in v1:
time: 263 us
  waiting for transfers between devices  134 us (51%)
  blocking collectives  46.3 us (18%)
  local copies, waits for them, and re-layouts  23.8 us (9%)
  other arithmetic  23.1 us (9%)
  between operations  15.1 us (6%)
  starting transfers between devices  11.9 us (5%)
  matrix products  8.56 us (3%)
    psum x2, waiting for transfers between devices, create_cube(): return lax.psum(lax.psum(a0, axis_name=shard_axis), mesh_name)  122 us
    psum x2, blocking collectives, create_cube(): return lax.psum(lax.psum(a0, axis_name=shard_axis), mesh_name)  36.4 us
    all_to_all x1, blocking collectives, body(): lax.all_to_all(outgoing.astype(jnp.bfloat16), ('section', 'view'), split_...  9.91 us
    all_to_all x1, starting transfers between devices, body(): lax.all_to_all(wanted_rows, ('section', 'view'), split_axis=0, concat_axi...  8.34 us
    all_to_all x1, waiting for transfers between devices, body(): lax.all_to_all(answer, ('section', 'view'), split_axis=0, concat_axis=0,...  7.22 us
    scatter-add x1, other arithmetic, body(): own = jnp.zeros((PARAMS, own_count), jnp.float32).at[:, asked.reshape(-1)...  6.72 us
    add x1, other arithmetic, body(): sorted_owner * bucket + rank  5.71 us
  transfers between devices with their start and end apart: 4, of which 4 were waited for; matrix products, arithmetic and copies ran while one was open for 1% of the time, Pallas kernels for 0%

profile of v1, /device:TPU:0, one launch (start us, length us, event | category | flops | bytes accessed | tf_op | source)
XLA Modules:
  0.0 262.6 jit_solution(14201487273805411756)
XLA Ops:
  7.2 0.8 bitcast_subtract_fusion
  8.0 0.1 convert_reduce_fusion
  8.1 3.8 %sort.17 = (s32[512]{0:T(512)}, s32[512]{0:T(512)S(1)}) sort(s32[512]{0:T(512)S(1)} %get-tuple-element.51, s32[512]{0:T(512)S(1)} %iota.50), dimensions={0}, to_apply=%region_0.0 | sort | flops 4608 | bytes 8192 | tf_op jit(solution)/shard_map/jit(argsort)/sort | solution.py:85
  11.9 3.5 %gather_fusion = s32[512]{0:T(512)S(1)} fusion(s32[512]{0:T(512)S(1)} %get-tuple-element.51, s32[1024]{0:T(1024)S(1)} %pad_clamp_fusion.1), kind=kCustom, calls=%fused_computation | custom fusion | bytes 6144 | tf_op jit(solution)/shard_map/gather | solution.py:86
  15.4 0.1 copy.121
  15.6 0.1 reduce.3
  15.7 0.7 fusion.106
  16.4 4.3 %compare_select_fusion.3 = (s32[512,1]{0,1:T(1,128)S(1)}, s32[512,1]{0,1:T(1,128)S(1)}) fusion(s32[]{:T(128)} %bitcast.12, s32[]{:T(128)} %bitcast.13, s32[]{:T(128)} %bitcast.14, s32[]{:T(128)} %bitcast.15, s32[]{:T(128)} %bitcast.16, s32[]{:T(128)} %bitcast.18, s32[]{:T(128)} %bitcast.17, s32[512,1]{0,1:T(1,128)S(1)} %bitcast.179), kind=kLoop, calls=%fused_computation.113 | loop fusion | flops 7680 | bytes 6172 | tf_op jit(solution)/shard_map/gather | solution.py:90
  20.7 0.1 compare_reduce_fusion.8
  20.8 5.7 %fusion.82 = s32[512]{0:T(512)S(1)} fusion(pred[512]{0:T(512)(128)(4,1)S(1)} %get-tuple-element.25, pred[512]{0:T(512)(128)(4,1)S(1)} %get-tuple-element.24, pred[512]{0:T(512)(128)(4,1)S(1)} %get-tuple-element.23, pred[512]{0:T(512)(128)(4,1)S(1)} %get-tuple-element.22, pred[512]{0:T(512)(128)(4,1)S(1)} %get-tuple-element.21, ...), kind=kLoop, calls=%fused_computation.148 | loop fusion | flops 6144 | bytes 10788 | tf_op jit(solution)/shard_map/add | solution.py:91
  26.5 2.4 scatter_custom_fusion
  29.0 2.4 scatter_custom_fusion.1
  31.4 0.7 all_to_all.12
  32.1 8.3 %all-to-all-start = ((s32[16,1,64]{2,1,0:T(1,128)}), s32[16,1,64]{2,1,0:T(1,128)S(1)}, u32[]{:S(2)}, u32[]{:S(2)}) async-start(s32[16,1,64]{2,1,0:T(1,128)} %all_to_all.12), calls=%async_computation | async-start | bytes 16384 | tf_op jit(solution)/shard_map/all_to_all | solution.py:95
  40.5 0.1 fusion.86
  40.6 0.1 fusion.87
  40.7 0.1 fusion.54
  40.8 0.2 fusion.85
  41.0 0.3 slice_reduce_fusion.7
  41.3 0.5 copy.122
  41.9 0.6 fusion.4
  42.5 0.3 copy.142
  42.8 4.9 %all-to-all-done = s32[16,1,64]{2,1,0:T(1,128)S(1)} async-done(((s32[16,1,64]{2,1,0:T(1,128)}), s32[16,1,64]{2,1,0:T(1,128)S(1)}, u32[]{:S(2)}, u32[]{:S(2)}) %all-to-all-start) | async-done | bytes 4128 | tf_op jit(solution)/shard_map/all_to_all | solution.py:95
  47.7 0.5 broadcast.1157
  48.2 0.7 reduce.40
  48.9 0.1 reshape.1626
  49.0 3.2 %gather_fusion.1 = bf16[1024,8]{1,0:T(8,128)(2,1)S(1)} fusion(bf16[8,2048]{0,1:T(8,128)(2,1)S(1)} %bitcast.162, s32[1024]{0:T(1024)S(1)} %broadcast_clamp_fusion), kind=kCustom, calls=%fused_computation.1 | custom fusion | bytes 36864 | tf_op jit(solution)/shard_map/jit(_take)/gather | solution.py:101
  52.2 0.1 copy.124
  52.4 0.7 reshape.1807
  53.1 3.5 %all-to-all-start.1 = ((bf16[16,2,256]{2,1,0:T(2,128)(2,1)}), bf16[16,2,256]{2,1,0:T(2,128)(2,1)S(1)}, u32[]{:S(2)}, u32[]{:S(2)}) async-start(bf16[16,2,256]{2,1,0:T(2,128)(2,1)} %reshape.1807), calls=%async_computation.1 | async-start | bytes 32768 | tf_op jit(solution)/shard_map/all_to_all | solution.py:105
  56.6 0.0 all-reduce.12.cloned.1.call-start
  56.7 7.2 %all-to-all-done.1 = bf16[16,2,256]{2,1,0:T(2,128)(2,1)S(1)} async-done(((bf16[16,2,256]{2,1,0:T(2,128)(2,1)}), bf16[16,2,256]{2,1,0:T(2,128)(2,1)S(1)}, u32[]{:S(2)}, u32[]{:S(2)}) %all-to-all-start.1) | async-done | bytes 16416 | tf_op jit(solution)/shard_map/all_to_all | solution.py:105
  63.9 0.1 reshape.1808
  64.0 0.2 copy.125
  64.2 1.0 gather_fusion.2
  65.2 0.1 copy.126
  65.4 0.1 add_tanh_fusion.1
  65.5 0.9 convolution_exponential_fusion
  66.4 1.3 multiply_reduce_fusion
  67.7 0.9 fusion.52
  68.6 0.7 fusion.65
  69.3 1.6 fusion.19
  70.9 0.1 broadcast_multiply_fusion.6
  71.0 0.1 broadcast_multiply_fusion.1
  71.1 0.1 copy.134
  71.3 1.8 scatter_custom_fusion.2
  73.1 0.1 copy.135
  73.3 0.1 reshape.1809
  73.4 9.9 %all_to_all.19 = bf16[16,2,256]{2,1,0:T(2,128)(2,1)S(1)} all-to-all(bf16[16,2,256]{2,1,0:T(2,128)(2,1)S(1)} %reshape.1809), channel_id=1, replica_groups=mesh['section'=2,'view'=8,'scene'=2] {'section','view'}, dimensions={0} | all-to-all | bytes 32768 | tf_op jit(solution)/shard_map/all_to_all | solution.py:128
  83.3 0.1 reshape.1810
  83.4 0.1 reshape.1711
  83.5 0.2 copy.137
  83.7 6.7 %scatter_custom_fusion.3 = f32[8,2048]{0,1:T(8,128)S(1)} fusion(s32[1024]{0:T(1024)S(1)} %bitcast.181, f32[1024,8]{1,0:T(8,128)S(1)} %copy.137, f32[]{:T(128)} %constant.123.clone.1), kind=kCustom, calls=%fused_computation.48 | custom fusion | flops 8192 | bytes 65540 | tf_op jit(solution)/shard_map/scatter-add | solution.py:134
  90.4 0.3 copy.138
  90.8 0.1 reshape.1631
  90.9 2.4 fusion.58
  93.3 0.0 all-reduce.12.cloned.1.call-update
  93.3 0.0 all-reduce.14.cloned.1.call-start
  93.3 94.7 %all-reduce.12.cloned.1.call-done = f32[1024,512]{1,0:T(8,128)} async-done(((f32[1024,512]{1,0:T(8,128)}), f32[1024,512]{1,0:T(8,128)}) %all-reduce.12.cloned.1.call-update) | async-done | bytes 2097168 | tf_op jit(solution)/shard_map/psum | solution.py:14
  188.7 30.9 %psum.30 = f32[]{:T(128)} all-reduce(f32[]{:T(128)S(6)} %mul.699), channel_id=1, replica_groups=mesh['section'=2,'view'=8,'scene'=2] {'view','scene'}, use_global_device_ids=true, to_apply=%region_15.16 | all-reduce | flops 1 | bytes 8 | tf_op jit(solution)/shard_map/psum | solution.py:14
  219.6 5.5 %psum.31 = f32[]{:T(128)} all-reduce(f32[]{:T(128)} %psum.30), channel_id=1, replica_groups=mesh['section'=2,'view'=8,'scene'=2] {'section'}, use_global_device_ids=true, to_apply=%region_16.17 | all-reduce | flops 1 | bytes 8 | tf_op jit(solution)/shard_map/psum | solution.py:14
  225.1 0.6 convert_element_type.110
  225.7 26.9 %all-reduce.14.cloned.1.call-done = f32[1024,512]{1,0:T(8,128)} async-done(((f32[1024,512]{1,0:T(8,128)}), f32[1024,512]{1,0:T(8,128)}) %all-reduce.14.cloned.1.call-update) | async-done | bytes 2097168 | tf_op jit(solution)/shard_map/psum | solution.py:14
  252.7 3.1 %copy.159 = f32[1024,512]{1,0:T(8,128)} copy(f32[1024,512]{1,0:T(8,128)} %all-reduce.14.cloned.1.call-done) | data formatting | bytes 4194304
  (43 shorter events, 0.4 us)
Async XLA Ops:
  7.2 33.6 %copy-start = (f32[1,2,8]{2,1,0:T(2,128)S(1)}, f32[1,2,8]{2,1,0:T(2,128)}, u32[]{:S(2)}) copy-start(f32[1,2,8]{2,1,0:T(2,128)} %param.12) | copy-start | bytes 196
  7.2 33.3 %copy-start.5 = (s32[1,4]{1,0:T(1,128)S(1)}, s32[1,4]{1,0:T(1,128)}, u32[]{:S(2)}) copy-start(s32[1,4]{1,0:T(1,128)} %param.11) | copy-start | bytes 52
  7.2 33.5 %copy-start.2 = (bf16[1,32,1024]{2,1,0:T(8,128)(2,1)S(1)}, bf16[1,32,1024]{2,1,0:T(8,128)(2,1)}, u32[]{:S(2)}) copy-start(bf16[1,32,1024]{2,1,0:T(8,128)(2,1)} %param.7) | copy-start | bytes 196612
  7.2 34.1 %copy-start.1 = (bf16[1024,512]{1,0:T(8,128)(2,1)S(1)}, bf16[1024,512]{1,0:T(8,128)(2,1)}, u32[]{:S(2)}) copy-start(bf16[1024,512]{1,0:T(8,128)(2,1)} %param.9) | copy-start | bytes 3145732
  11.9 30.0 %copy-start.3 = (f32[1024]{0:T(1024)S(1)}, f32[1024]{0:T(1024)}, u32[]{:S(2)}) copy-start(f32[1024]{0:T(1024)} %param.8) | copy-start | bytes 12292
  32.1 15.6 %all-to-all-start = ((s32[16,1,64]{2,1,0:T(1,128)}), s32[16,1,64]{2,1,0:T(1,128)S(1)}, u32[]{:S(2)}, u32[]{:S(2)}) async-start(s32[16,1,64]{2,1,0:T(1,128)} %all_to_all.12), calls=%async_computation | async-start | bytes 16384 | tf_op jit(solution)/shard_map/all_to_all | solution.py:95
  41.3 15.3 %copy-start.4 = (bf16[1,4,768]{2,1,0:T(4,128)(2,1)S(1)}, bf16[1,4,768]{2,1,0:T(4,128)(2,1)}, u32[]{:S(2)}) copy-start(bf16[1,4,768]{2,1,0:T(4,128)(2,1)} %param.13) | copy-start | bytes 18436
  53.1 10.8 %all-to-all-start.1 = ((bf16[16,2,256]{2,1,0:T(2,128)(2,1)}), bf16[16,2,256]{2,1,0:T(2,128)(2,1)S(1)}, u32[]{:S(2)}, u32[]{:S(2)}) async-start(bf16[16,2,256]{2,1,0:T(2,128)(2,1)} %reshape.1807), calls=%async_computation.1 | async-start | bytes 32768 | tf_op jit(solution)/shard_map/all_to_all | solution.py:105
  56.6 131.4 %all-reduce.12.cloned.1.call-start = ((), (), s32[]{:S(2)}) async-start(), calls=%async_computation.3 | async-start | bytes 4194304 | tf_op jit(solution)/shard_map/psum | solution.py:14
  93.3 159.4 %all-reduce.14.cloned.1.call-start = ((), (), s32[]{:S(2)}) async-start(), calls=%async_computation.4 | async-start | bytes 4194304 | tf_op jit(solution)/shard_map/psum | solution.py:14
Sparse Core Ops, SparseCore 0:
  93.4 94.5 all-reduce.11
  190.3 62.3 all-reduce.13
